TPU v7x, 256 devices: a whole 4x4x8 slice. The times are simulated.
256 devices in a mesh: mom: 16 (over z, x_lo), en: 16 (over x_hi, y, core).
Axes of the slice: x: 4 (x_hi: 2, x_lo: 2; x = x_hi * 2 + x_lo), y: 4, z: 8, core: 2. Of those that a mesh axis runs over, the one named last changes fastest.
Arguments:
- greens: bfloat16 [32, 2, 2, 12, 12, 2048], P('mom', None, None, None, None, 'en'), may hold values from -6 to 6
- phonon_kernel: bfloat16 [32, 2, 2, 16], replicated, may hold values from -0.1875 to 0.1875
- coupling: bfloat16 [2, 2, 12, 12], replicated, may hold values from -1.75 to 1.75
- neighbours: int32 [2, 2], replicated, may hold values from 0 to 1
- transfer_table: int32 [32, 32], replicated, may hold values from 0 to 31, as said below
Outputs:
- self_energy: bfloat16 [32, 2, 2, 12, 12, 2048], P('mom', None, None, None, None, 'en')
Inputs may be any that keep to these rules, and one draw needn't show every extreme that they name: `transfer_table`: every row and every column of the table holds each of 0 to 31 once.
All inputs are finite; a program needn't handle non-finite values.
Results may differ from a plain program's by a relative error of at most 0.0058.
Values may be sent and summed in bfloat16 or wider, within the bound.
A program may use at most 64 MiB of HBM per device.

v0:
```python
import jax
import jax.numpy as jnp
from jax import lax
from jax.sharding import Mesh
from jax.sharding import PartitionSpec as P

MOM = ("mom_0", "mom_1")


def from_behind(block, axis, distance):
    devices = range(lax.axis_size(axis))
    route = [(i - distance, i) for i in devices if i - distance in devices]
    return lax.ppermute(block, axis, route)


def whole_of(value, axes, dim):
    if not axes:
        return value
    nearer = lax.all_gather(value, axes[-1], axis=dim, tiled=True)
    return whole_of(nearer, axes[:-1], dim)


def couple(green_block, neighbours, coupling):
    collected_blocks = jnp.take(green_block, neighbours, axis=0)
    half_width = jnp.einsum(
        "anop,anrpse->anrose", coupling, collected_blocks, preferred_element_type=jnp.float32
    ).astype(jnp.bfloat16)
    full = jnp.einsum(
        "qbiwjm,qbkj->qbiwkm", half_width, coupling, preferred_element_type=jnp.float32
    ).astype(jnp.bfloat16)
    return full.reshape(full.shape[0], full.shape[1], -1, full.shape[-1])


def local(greens, phonon_kernel, coupling, neighbours, transfer_table):
    kcount, local_atom_count, parts, orbits, _, energies = greens.shape
    lag_count = phonon_kernel.shape[-1]
    extent = energies + lag_count - 1
    energy_lag_index = jnp.arange(lag_count)[:, None, None]
    column_index = jnp.arange(extent)[None, :, None]
    energy_index = jnp.arange(energies)[None, None, :]
    lag_table = (column_index == energy_index + lag_count - 1 - energy_lag_index).astype(
        jnp.bfloat16
    )
    upper_border = greens[..., energies - (lag_count - 1) :]
    lower_rim = from_behind(upper_border, "en", 1)
    extended = jnp.concatenate([lower_rim, greens], axis=-1)
    first_row = lax.axis_index(MOM) * kcount
    out_shape = (local_atom_count, parts, orbits, orbits, energies)
    start_sum = jnp.zeros((kcount,) + out_shape, jnp.float32)
    shard_piece = whole_of(extended, MOM, 0)

    def absorb_one(index_in, running_partial_sum):
        green_block = lax.dynamic_index_in_dim(shard_piece, index_in, 0, keepdims=False)
        weights = couple(green_block, neighbours, coupling)
        column = lax.dynamic_index_in_dim(transfer_table, index_in, 1, keepdims=False)
        transfers = lax.dynamic_slice_in_dim(column, first_row, kcount, 0)
        kernels = jnp.take(phonon_kernel, transfers, axis=0)
        matrix = jnp.einsum(
            "kanl,lje->kanje", kernels, lag_table, preferred_element_type=jnp.float32
        ).astype(jnp.bfloat16)
        term = jnp.einsum("anxj,kanje->kaxe", weights, matrix, preferred_element_type=jnp.float32)
        return running_partial_sum + term.reshape((kcount,) + out_shape)

    summed = lax.fori_loop(0, shard_piece.shape[0], absorb_one, start_sum)
    return summed.astype(jnp.bfloat16)


def solution(mesh):
    finer = Mesh(mesh.devices.reshape(8, 2, mesh.shape["en"]), ("mom_0", "mom_1", "en"))
    return jax.shard_map(
        local,
        mesh=finer,
        in_specs=(P(MOM, None, None, None, None, "en"), P(), P(), P(), P()),
        out_specs=P(MOM, None, None, None, None, "en"),
        check_vma=False,
    )
```

profile of v0, /device:TPU:1, one launch (start us, length us, event | category | flops | bytes accessed | tf_op | source)
XLA Modules:
  0.0 376.5 jit_solution(5154154687651916680)
XLA Ops:
  7.9 4.6 %collective-permute-start = (bf16[2,2,2,12,12,15]{5,2,4,3,1,0:T(2,128)(2,1)S(1)}, bf16[2,2,2,12,12,15]{5,2,4,3,1,0:T(2,128)(2,1)S(1)}, u32[]{:S(2)}, u32[]{:S(2)}) collective-permute-start(bf16[2,2,2,12,12,15]{5,2,4,3,1,0:T(2,128)(2,1)S(1)} %slice.3), channel_id=1, source_target_pairs={{0,1},{1,2},{2,3},{3,4},{4,5},{5,6},{6,7},{7,8},{8,9},{9,10},{10,1... | collective-permute-start | bytes 103688 | tf_op jit(solution)/shard_map/ppermute | solution.py:13
  12.5 3.6 collective-permute-done
  16.1 2.1 pad_maximum_fusion
  18.2 13.9 %all_gather.6 = bf16[4,2,2,12,12,143]{5,2,4,3,1,0:T(2,128)(2,1)} all-gather(bf16[2,2,2,12,12,143]{5,2,4,3,1,0:T(2,128)(2,1)S(1)} %pad_maximum_fusion), channel_id=1, replica_groups=mesh['mom_0'=8,'mom_1'=2,'en'=16] {'mom_1'}, dimensions={0}, use_global_device_ids=true | all-gather | bytes 988416 | tf_op jit(solution)/shard_map/all_gather | solution.py:19
  32.4 108.4 %all-gather.2.cloned.1.call-done = bf16[32,2,2,12,12,143]{5,2,4,3,1,0:T(2,128)(2,1)} async-done(((bf16[4,2,2,12,12,143]{5,2,4,3,1,0:T(2,128)(2,1)}), bf16[32,2,2,12,12,143]{5,2,4,3,1,0:T(2,128)(2,1)}) %all-gather.2.cloned.1.call-update) | async-done | bytes 5271568 | tf_op jit(solution)/shard_map/all_gather | solution.py:19
  140.8 227.7 %while.17 = (s32[]{:T(128)}, f32[2,2,2,12,12,128]{5,1,4,3,2,0:T(2,128)S(1)}, s32[32,32]{0,1:T(8,128)S(1)}, s32[]{:T(128)}, bf16[32,2,2,16]{3,2,1,0:T(2,128)(2,1)...) while((s32[]{:T(128)}, ...), condition=%wide.region_1.2_spmd.clone, body=%wide.region_0.1_spmd.clone.sunk | while | flops 98461488 | bytes 7439167 | solution.py:64
  142.1 1.7 gather_fusion
  149.2 1.7 gather_fusion
  156.3 1.7 gather_fusion
  163.4 1.7 gather_fusion
  170.5 1.7 gather_fusion
  177.7 1.7 gather_fusion
  184.8 1.7 gather_fusion
  191.9 1.7 gather_fusion
  199.0 1.7 gather_fusion
  206.1 1.7 gather_fusion
  213.2 1.7 gather_fusion
  220.4 1.7 gather_fusion
  227.5 1.7 gather_fusion
  234.6 1.7 gather_fusion
  312.9 1.7 gather_fusion
  327.1 1.7 gather_fusion
  341.3 1.7 gather_fusion
  355.6 1.7 gather_fusion
  (512 shorter events, 196.2 us)
Async XLA Ops:
  6.5 134.3 %all-gather.2.cloned.1.call-start = ((), (), s32[]{:S(2)}) async-start(), calls=%async_computation | async-start | bytes 10616832 | tf_op jit(solution)/shard_map/all_gather | solution.py:19
  7.9 8.2 %collective-permute-start = (bf16[2,2,2,12,12,15]{5,2,4,3,1,0:T(2,128)(2,1)S(1)}, bf16[2,2,2,12,12,15]{5,2,4,3,1,0:T(2,128)(2,1)S(1)}, u32[]{:S(2)}, u32[]{:S(2)}) collective-permute-start(bf16[2,2,2,12,12,15]{5,2,4,3,1,0:T(2,128)(2,1)S(1)} %slice.3), channel_id=1, source_target_pairs={{0,1},{1,2},{2,3},{3,4},{4,5},{5,6},{6,7},{7,8},{8,9},{9,10},{10,1... | collective-permute-start | bytes 103688 | tf_op jit(solution)/shard_map/ppermute | solution.py:13
  18.2 14.0 %copy-start.2 = (s32[32,32]{1,0:T(8,128)S(1)}, s32[32,32]{1,0:T(8,128)}, u32[]{:S(2)}) copy-start(s32[32,32]{1,0:T(8,128)} %param.11) | copy-start | bytes 12292
  18.2 14.0 %copy-start.1 = (bf16[32,2,2,16]{0,3,2,1:T(8,128)(2,1)S(1)}, bf16[32,2,2,16]{0,3,2,1:T(8,128)(2,1)}, u32[]{:S(2)}) copy-start(bf16[32,2,2,16]{0,3,2,1:T(8,128)(2,1)} %param.8) | copy-start | bytes 12292
  18.2 14.1 %copy-start.3 = (bf16[2,2,12,12]{3,1,2,0:T(2,128)(2,1)S(1)}, bf16[2,2,12,12]{3,1,2,0:T(2,128)(2,1)}, u32[]{:S(2)}) copy-start(bf16[2,2,12,12]{3,1,2,0:T(2,128)(2,1)} %param.9) | copy-start | bytes 3460
  18.2 122.6 %copy-start = (s32[2,2]{1,0:T(2,128)S(1)}, s32[2,2]{1,0:T(2,128)}, u32[]{:S(2)}) copy-start(s32[2,2]{1,0:T(2,128)} %param.10) | copy-start | bytes 52
Sparse Core Ops, SparseCore 0:
  32.3 108.5 all-gather.1
where the time goes:
time: 378 us; the launch traced here: 377 us
  local copies, waits for them, and re-layouts  151 us (40%)
  waiting for transfers between devices  112 us (30%)
  matrix products  48.5 us (13%)
  other arithmetic  30.4 us (8%)
  blocking collectives  13.9 us (4%)
  between operations  13.5 us (4%)
  starting transfers between devices  4.59 us (1%)
    all_gather x1, waiting for transfers between devices, whole_of(): nearer = lax.all_gather(value, axes[-1], axis=dim, tiled=True)  108 us
    gather x32, local copies, waits for them, and re-layouts, couple(): collected_blocks = jnp.take(green_block, neighbours, axis=0)  55.4 us
    squeeze x32, local copies, waits for them, and re-layouts, absorb_one(): lax.dynamic_index_in_dim(shard_piece, index_in, 0, keepdims=False)  37.4 us
    add x32, other arithmetic, absorb_one(): return running_partial_sum + term.reshape((kcount,) + out_shape)  24.7 us
    convert_element_type x32, local copies, waits for them, and re-layouts, couple(): full = jnp.einsum('qbiwjm,qbkj->qbiwkm', half_width, coupling, preferred_...  19.5 us
    gather x32, local copies, waits for them, and re-layouts, absorb_one(): kernels = jnp.take(phonon_kernel, transfers, axis=0)  18.3 us
    transpose x32, local copies, waits for them, and re-layouts, absorb_one(): jnp.einsum('anxj,kanje->kaxe', weights, matrix, preferred_element_type=jn...  14.6 us
    all_gather x1, blocking collectives, whole_of(): nearer = lax.all_gather(value, axes[-1], axis=dim, tiled=True)  13.9 us
  transfers between devices with their start and end apart: 2, of which 2 were waited for; matrix products, arithmetic and copies ran while one was open for 0% of the time, Pallas kernels for 0%

commit v1 on v0

v1 whole, which is shorter than its diff:
```python
import functools

import jax
import jax.numpy as jnp
from jax import lax
from jax.experimental import pallas as pl
from jax.experimental.pallas import tpu as pltpu
from jax.sharding import PartitionSpec as P

MESH = pl.DeviceIdType.MESH
F32 = jnp.float32
BF16 = jnp.bfloat16
I32 = jnp.int32

ORB = 12
PAIRS = 144
HALF = 72
WIDE = 128
ORDER = (
    (4, 0), (3, 1), (5, 0), (2, 1), (4, 1), (6, 0), (3, 0), (5, 1),
    (2, 0), (6, 1), (1, 1), (7, 0), (1, 0), (7, 1), (0, 1),
)


def lane(shape):
    return lax.broadcasted_iota(I32, shape, len(shape) - 1)


def row(shape):
    return lax.broadcasted_iota(I32, shape, len(shape) - 2)


def pick(index, choices):
    out = choices[-1]
    for value in range(len(choices) - 2, -1, -1):
        out = jnp.where(index == value, choices[value], out)
    return out


def dot(a, b):
    return jnp.dot(a, b, preferred_element_type=F32)


def dot_t(a, b):
    return lax.dot_general(a, b, (((1,), (1,)), ((), ())), preferred_element_type=F32)


def kernel(
    nen, g_ref, ph_ref, c_ref, nb_ref, t_ref, out_ref,
    yt, send1, recv1, rim_out, rim_in, ga, tt, ohs, t0, kron, send2, recv2,
    send1_sem, recv1_sem, send2_sem, recv2_sem, rim_sems, local_sems,
):
    m = lax.axis_index("mom")
    q = lax.axis_index("en")
    z = m // 2
    x = m % 2
    up = lax.rem(q + 1, nen)
    down = lax.rem(q + nen - 1, nen)

    def peer(step):
        dz, dx = step
        return lax.rem(z + dz, 8) * 2 + lax.rem(x + dx, 2)

    barrier = pltpu.get_barrier_semaphore()
    for step in ORDER:
        pl.semaphore_signal(barrier, inc=1, device_id={"mom": peer(step)}, device_id_type=MESH)
    pl.semaphore_signal(barrier, inc=1, device_id={"en": up}, device_id_type=MESH)
    pl.semaphore_signal(barrier, inc=1, device_id={"en": down}, device_id_type=MESH)

    for r in range(2):
        for c in range(4):
            block = g_ref.at[c % 2, lax.rem(c // 2 + x, 2), r]
            for o in range(ORB):
                piece = block[o].astype(F32)
                if c:
                    piece = pltpu.roll(piece, 32 * c, 1)
                yt[r, c, o * ORB : (o + 1) * ORB, :] = piece

    place = lane((PAIRS, WIDE)) >> 4

    def packed(b, r):
        return pick(((place + (9 - b)) & 7) >> 1, [yt[r, c] for c in range(4)])

    odd = (place & 1) == 1
    first = [packed(0, r) for r in range(2)]
    rim_out[...] = jnp.where(odd, first[0], pltpu.roll(first[1], 16, 1)).astype(BF16)
    for r in range(2):
        send1[r] = first[r].astype(BF16)

    pl.semaphore_wait(barrier, 17)
    rim = pltpu.make_async_remote_copy(
        rim_out, rim_in, rim_sems.at[0], rim_sems.at[1], device_id={"en": up}, device_id_type=MESH
    )
    rim.start()

    for b in range(1, 8):
        for r in range(2):
            send1[2 * b + r] = packed(b, r).astype(BF16)

    rim.wait()
    below = jnp.where(q > 0, rim_in[...].astype(F32), 0.0)
    for r in range(2):
        part = below if r == 0 else pltpu.roll(below, WIDE - 16, 1)
        send1[r] = jnp.where(odd, part, send1[r].astype(F32)).astype(BF16)

    def leg(step, send, recv, send_sem, recv_sem):
        there = peer(step)
        return pltpu.make_async_remote_copy(
            send.at[there], recv.at[m], send_sem.at[there], recv_sem.at[m],
            device_id={"mom": there}, device_id_type=MESH,
        )

    def arrival(step, send, recv, send_sem, recv_sem):
        there = peer(step)
        return pltpu.make_async_remote_copy(
            send.at[there], recv.at[there], send_sem.at[there], recv_sem.at[there],
            device_id={"mom": there}, device_id_type=MESH,
        )

    leg1 = (send1, recv1, send1_sem, recv1_sem)
    leg2 = (send2, recv2, send2_sem, recv2_sem)
    for step in ORDER:
        leg(step, *leg1).start()
    own1 = pltpu.make_async_copy(send1.at[m], recv1.at[m], local_sems.at[0])
    own1.start()

    table = t_ref[...].astype(F32).astype(BF16)
    kk = row((32, WIDE))
    for v in range(2):
        for g in range(8):
            slot = lane((32, WIDE)) >> 5
            if v:
                slot = slot ^ 2
            spread = (kk == slot + 4 * g).astype(F32).astype(BF16)
            wanted = (lane((32, WIDE)) & 31).astype(F32)
            ohs[v, g * 32 : (g + 1) * 32, :] = (dot(table, spread) == wanted).astype(F32).astype(BF16)

    shifted = (lane((WIDE, WIDE)) - 16 * (z + 7)) & 127
    slot_match = (row((WIDE, WIDE)) >> 5) == (shifted >> 5)
    lag_at = ((lane((64, WIDE)) - 16 * (z + 7)) & 31)
    for an in range(4):
        select = jnp.where(row((64, WIDE)) == 16 * an + 16 - lag_at, 1.0, 0.0)
        select = jnp.where(lag_at == 0, 0.0, jnp.where(lag_at > 16, 0.0, select)).astype(BF16)
        lags = dot(ph_ref[...], select)
        lags = jnp.concatenate([lags] * 4, axis=0)
        lags = jnp.where(slot_match, lags, 0.0).astype(BF16)
        t0[an] = dot(ohs[nb_ref[an // 2, an % 2]], lags)

    def spread_rows(k, carry):
        at = pl.multiple_of((k // 8) * 128 + lax.rem(k + z, 8) * 16, 16)
        for an in range(4):
            for g in range(8):
                line = jnp.broadcast_to(t0[an, pl.ds(g * 32 + k, 1), :], (16, WIDE))
                line = pltpu.roll(line, 0, 1, stride=1, stride_axis=0)
                tt[an, pl.ds(at, 16), g * WIDE : (g + 1) * WIDE] = line.astype(BF16)
        return carry

    lax.fori_loop(0, 32, spread_rows, 0)

    high = row((PAIRS, ORB))
    small = lane((PAIRS, ORB))
    over = jnp.zeros((PAIRS, ORB), I32)
    for i in range(1, ORB):
        over += (high >= ORB * i).astype(I32)
    outer = (over == small).astype(F32).astype(BF16)
    inner = (high - ORB * over == small).astype(F32).astype(BF16)
    for an in range(4):
        block = c_ref[an // 2, an % 2]
        left = dot_t(dot(outer, block).astype(BF16), outer)
        right = dot_t(dot(inner, block).astype(BF16), inner)
        kron[an] = (left * right).astype(BF16)

    own1.wait()
    for step in ORDER:
        arrival(step, *leg1).wait_recv()

    lower = (((lane((PAIRS, WIDE)) - 16 * (z + 7)) & 127) < 64)
    for g in range(8):
        near = recv1[2 * g].astype(F32)
        far = recv1[2 * g + 1].astype(F32)
        ga[0, :, g * WIDE : (g + 1) * WIDE] = jnp.where(lower, near, far).astype(BF16)
        ga[1, :, g * WIDE : (g + 1) * WIDE] = jnp.where(lower, far, near).astype(BF16)

    done = []
    for a in range(2):
        total = None
        for n in range(2):
            an = 2 * a + n
            conv = dot_t(ga[nb_ref[a, n]], tt[an]).astype(BF16)
            term = dot(kron[an], conv)
            total = term if total is None else total + term
        done.append(total)

    place2 = lane((HALF, WIDE)) >> 4
    for g in range(4):
        tiles = []
        for c in range(4):
            tile = done[c % 2][HALF * (c // 2) : HALF * (c // 2 + 1), g * WIDE : (g + 1) * WIDE]
            tiles.append(pltpu.roll(tile, 32 * c, 1) if c else tile)
        for i in range(4):
            send2[4 * g + i] = pick(((place2 + 16 - z - 2 * i) & 7) >> 1, tiles).astype(BF16)

    for step in ORDER:
        leg(step, *leg2).start()
    own2 = pltpu.make_async_copy(send2.at[m], recv2.at[m], local_sems.at[1])
    own2.start()
    own2.wait()
    for step in ORDER:
        arrival(step, *leg2).wait_recv()

    mine = lax.rem(m, 4)
    for r in range(2):
        blocks = [recv2[2 * b + r].astype(F32) for b in range(8)]
        halves = []
        for c in range(8):
            merged = pick((place2 + 16 - c - 2 * mine) & 7, blocks)
            halves.append(pltpu.roll(merged, (16 * (16 - c - 2 * mine)) & 127, 1))
        for a in range(2):
            for k in range(2):
                whole = jnp.concatenate([halves[2 * a + k], halves[4 + 2 * a + k]], axis=0)
                out_ref[k, a, r] = whole.astype(BF16)

    for step in ORDER:
        leg(step, *leg1).wait_send()
        leg(step, *leg2).wait_send()


def local(greens, phonon_kernel, coupling, neighbours, transfer_table, *, nen):
    vmem = pl.BlockSpec(memory_space=pltpu.VMEM)
    out = pl.pallas_call(
        functools.partial(kernel, nen),
        out_shape=jax.ShapeDtypeStruct((2, 2, 2, PAIRS, WIDE), BF16),
        in_specs=[vmem, vmem, vmem, pl.BlockSpec(memory_space=pltpu.SMEM), vmem],
        out_specs=vmem,
        scratch_shapes=[
            pltpu.VMEM((2, 4, PAIRS, WIDE), F32),
            pltpu.VMEM((16, PAIRS, WIDE), BF16),
            pltpu.VMEM((16, PAIRS, WIDE), BF16),
            pltpu.VMEM((PAIRS, WIDE), BF16),
            pltpu.VMEM((PAIRS, WIDE), BF16),
            pltpu.VMEM((2, PAIRS, 8 * WIDE), BF16),
            pltpu.VMEM((4, 512, 8 * WIDE), BF16),
            pltpu.VMEM((2, 256, WIDE), BF16),
            pltpu.VMEM((4, 256, WIDE), F32),
            pltpu.VMEM((4, PAIRS, PAIRS), BF16),
            pltpu.VMEM((16, HALF, WIDE), BF16),
            pltpu.VMEM((16, HALF, WIDE), BF16),
            pltpu.SemaphoreType.DMA((16,)),
            pltpu.SemaphoreType.DMA((16,)),
            pltpu.SemaphoreType.DMA((16,)),
            pltpu.SemaphoreType.DMA((16,)),
            pltpu.SemaphoreType.DMA((2,)),
            pltpu.SemaphoreType.DMA((2,)),
        ],
        compiler_params=pltpu.CompilerParams(
            collective_id=0, has_side_effects=True, vmem_limit_bytes=32 * 2**20
        ),
    )(greens, phonon_kernel.reshape(32, 64), coupling, neighbours, transfer_table)
    return out.reshape(greens.shape)


def solution(mesh):
    spec = P("mom", None, None, None, None, "en")
    return jax.shard_map(
        functools.partial(local, nen=mesh.shape["en"]),
        mesh=mesh,
        in_specs=(spec, P(), P(), P(), P()),
        out_specs=spec,
        check_vma=False,
    )
```

time: 378 us -> 39.7 us (0.11)
  the two profiles are of different devices: /device:TPU:1 before, /device:TPU:16 now
where the time goes in v1:
time: 39.7 us; the launch traced here: 39.5 us
  Pallas kernels  36.7 us (92%)
  local copies, waits for them, and re-layouts  2.79 us (7%)
    pallas_call x1, Pallas kernels, local(): pl.pallas_call(functools.partial(kernel, nen), out_shape=jax.ShapeDtypeSt...  36.7 us
    unnamed x8, local copies, waits for them, and re-layouts  1.05 us
    pallas_call x1, local copies, waits for them, and re-layouts, local(): pl.pallas_call(functools.partial(kernel, nen), out_shape=jax.ShapeDtypeSt...  0.94 us
    reshape x1, local copies, waits for them, and re-layouts, local(): phonon_kernel.reshape(32, 64)  0.8 us

profile of v1, /device:TPU:16, one launch (start us, length us, event | category | flops | bytes accessed | tf_op | source)
XLA Modules:
  0.0 39.5 jit_solution(3029009696310138064)
XLA Ops:
  0.0 0.0 copy-start.2
  0.0 0.8 %copy.11.ph_ref = bf16[32,64]{1,0:T(8,128)(2,1)S(1)} copy(bf16[32,64]{0,1:T(8,128)(2,1)} %bitcast.2) | data formatting | bytes 8192 | tf_op jit(solution)/shard_map/reshape | solution.py:258
  0.8 0.0 copy-done.2
  0.8 0.0 copy-start
  0.8 0.0 copy-start.1
  0.8 1.0 %copy.10.g_ref = bf16[2,2,2,12,12,128]{5,4,3,2,1,0:T(8,128)(2,1)S(1)} copy(bf16[2,2,2,12,12,128]{5,2,4,3,1,0:T(2,128)(2,1)} %param.5) | data formatting | bytes 589824 | tf_op args[0]
  1.9 0.0 copy-done
  1.9 0.0 copy-done.1
  1.9 36.7 %shard_map.55 = bf16[2,2,2,144,128]{4,3,2,1,0:T(8,128)(2,1)S(1)} custom-call(bf16[2,2,2,12,12,128]{5,4,3,2,1,0:T(8,128)(2,1)S(1)} %copy.10.g_ref, bf16[32,64]{1,0:T(8,128)(2,1)S(1)} %copy.11.ph_ref, bf16[2,2,12,12]{3,2,1,0:T(8,128)(2,1)S(1)} %copy.12.c_ref, s32[2,2]{1,0:T(2,128)S(1)} %copy-done.1, s32[32,32]{1,0:T(8,128)S(1)} %copy-done), custom_call_target="tpu_custom_call" | custom-call | tf_op jit(solution)/shard_map/pallas_call | solution.py:230
  38.6 0.9 %copy.13 = bf16[2,2,2,144,128]{4,2,3,1,0:T(2,128)(2,1)} copy(bf16[2,2,2,144,128]{4,3,2,1,0:T(8,128)(2,1)S(1)} %shard_map.55) | data formatting | bytes 589824 | tf_op jit(solution)/shard_map/pallas_call | solution.py:230
  (1 shorter events, 0.0 us)
Async XLA Ops:
  0.0 0.8 %copy-start.2 = (bf16[2,2,12,12]{3,1,2,0:T(2,128)(2,1)S(1)}, bf16[2,2,12,12]{3,1,2,0:T(2,128)(2,1)}, u32[]{:S(2)}) copy-start(bf16[2,2,12,12]{3,1,2,0:T(2,128)(2,1)} %param.7) | copy-start | bytes 3460
  0.8 1.1 %copy-start = (s32[32,32]{1,0:T(8,128)S(1)}, s32[32,32]{1,0:T(8,128)}, u32[]{:S(2)}) copy-start(s32[32,32]{1,0:T(8,128)} %t_ref.1) | copy-start | bytes 12292
  0.8 1.1 %copy-start.1 = (s32[2,2]{1,0:T(2,128)S(1)}, s32[2,2]{1,0:T(2,128)}, u32[]{:S(2)}) copy-start(s32[2,2]{1,0:T(2,128)} %nb_ref.1) | copy-start | bytes 52

commit v2 on v1

--- a/solution.py
+++ b/solution.py
@@ -16,6 +16,7 @@
 PAIRS = 144
 HALF = 72
 WIDE = 128
+EARLY = 10
 ORDER = (
     (4, 0), (3, 1), (5, 0), (2, 1), (4, 1), (6, 0), (3, 0), (5, 1),
     (2, 0), (6, 1), (1, 1), (7, 0), (1, 0), (7, 1), (0, 1),
@@ -46,9 +47,10 @@
 
 
 def kernel(
-    nen, g_ref, ph_ref, c_ref, nb_ref, t_ref, out_ref,
-    yt, send1, recv1, rim_out, rim_in, ga, tt, ohs, t0, kron, send2, recv2,
-    send1_sem, recv1_sem, send2_sem, recv2_sem, rim_sems, local_sems,
+    nen, g_hbm, ph_hbm, c_hbm, nb_hbm, t_hbm, out_ref,
+    g_ref, ph_ref, c_ref, nb_ref, t_ref,
+    yt, send1, recv1, rim_out, rim_in, ga, tt, ohs, t0, kron, acc, send2, recv2,
+    send1_sem, recv1_sem, send2_sem, recv2_sem, rim_sems, local_sems, load_sems,
 ):
     m = lax.axis_index("mom")
     q = lax.axis_index("en")
@@ -67,14 +69,21 @@
     pl.semaphore_signal(barrier, inc=1, device_id={"en": up}, device_id_type=MESH)
     pl.semaphore_signal(barrier, inc=1, device_id={"en": down}, device_id_type=MESH)
 
-    for r in range(2):
-        for c in range(4):
-            block = g_ref.at[c % 2, lax.rem(c // 2 + x, 2), r]
-            for o in range(ORB):
-                piece = block[o].astype(F32)
-                if c:
-                    piece = pltpu.roll(piece, 32 * c, 1)
-                yt[r, c, o * ORB : (o + 1) * ORB, :] = piece
+    loads = [
+        pltpu.make_async_copy(there, here, load_sems.at[i])
+        for i, (there, here) in enumerate(
+            [(g_hbm, g_ref), (ph_hbm, ph_ref), (c_hbm, c_ref), (nb_hbm, nb_ref), (t_hbm, t_ref)]
+        )
+    ]
+    for load in loads:
+        load.start()
+    loads[0].wait()
+
+    for c in range(4):
+        both = g_ref[c % 2, lax.rem(c // 2 + x, 2)].astype(F32)
+        for r in range(2):
+            block = both[:, r, :]
+            yt[r, c] = pltpu.roll(block, 32 * c, 1) if c else block
 
     place = lane((PAIRS, WIDE)) >> 4
 
@@ -87,21 +96,12 @@
     for r in range(2):
         send1[r] = first[r].astype(BF16)
 
-    pl.semaphore_wait(barrier, 17)
     rim = pltpu.make_async_remote_copy(
         rim_out, rim_in, rim_sems.at[0], rim_sems.at[1], device_id={"en": up}, device_id_type=MESH
     )
-    rim.start()
-
     for b in range(1, 8):
         for r in range(2):
             send1[2 * b + r] = packed(b, r).astype(BF16)
-
-    rim.wait()
-    below = jnp.where(q > 0, rim_in[...].astype(F32), 0.0)
-    for r in range(2):
-        part = below if r == 0 else pltpu.roll(below, WIDE - 16, 1)
-        send1[r] = jnp.where(odd, part, send1[r].astype(F32)).astype(BF16)
 
     def leg(step, send, recv, send_sem, recv_sem):
         there = peer(step)
@@ -119,11 +119,8 @@
 
     leg1 = (send1, recv1, send1_sem, recv1_sem)
     leg2 = (send2, recv2, send2_sem, recv2_sem)
-    for step in ORDER:
-        leg(step, *leg1).start()
-    own1 = pltpu.make_async_copy(send1.at[m], recv1.at[m], local_sems.at[0])
-    own1.start()
-
+    for load in loads[1:]:
+        load.wait()
     table = t_ref[...].astype(F32).astype(BF16)
     kk = row((32, WIDE))
     for v in range(2):
@@ -138,13 +135,42 @@
     shifted = (lane((WIDE, WIDE)) - 16 * (z + 7)) & 127
     slot_match = (row((WIDE, WIDE)) >> 5) == (shifted >> 5)
     lag_at = ((lane((64, WIDE)) - 16 * (z + 7)) & 31)
+    same = (row((32, 32)) == lane((32, 32))).astype(F32).astype(BF16)
+    kernels = dot_t(same, ph_ref[...]).astype(BF16)
     for an in range(4):
         select = jnp.where(row((64, WIDE)) == 16 * an + 16 - lag_at, 1.0, 0.0)
         select = jnp.where(lag_at == 0, 0.0, jnp.where(lag_at > 16, 0.0, select)).astype(BF16)
-        lags = dot(ph_ref[...], select)
+        lags = dot(kernels, select)
         lags = jnp.concatenate([lags] * 4, axis=0)
         lags = jnp.where(slot_match, lags, 0.0).astype(BF16)
         t0[an] = dot(ohs[nb_ref[an // 2, an % 2]], lags)
+
+    pl.semaphore_wait(barrier, 17)
+    rim.start()
+    own1 = pltpu.make_async_copy(send1.at[m], recv1.at[m], local_sems.at[0])
+
+    def send_above(step):
+        @pl.when(lax.rem(z + step[0], 8) != 0)
+        def _():
+            leg(step, *leg1).start()
+
+    def send_lowest(step):
+        @pl.when(lax.rem(z + step[0], 8) == 0)
+        def _():
+            leg(step, *leg1).start()
+
+    for step in ORDER[:EARLY]:
+        send_above(step)
+    rim.wait()
+    below = jnp.where(q > 0, rim_in[...].astype(F32), 0.0)
+    for r in range(2):
+        part = below if r == 0 else pltpu.roll(below, WIDE - 16, 1)
+        send1[r] = jnp.where(odd, part, send1[r].astype(F32)).astype(BF16)
+    for step in ORDER:
+        send_lowest(step)
+    own1.start()
+    for step in ORDER[EARLY:]:
+        send_above(step)
 
     def spread_rows(k, carry):
         at = pl.multiple_of((k // 8) * 128 + lax.rem(k + z, 8) * 16, 16)
@@ -152,7 +178,7 @@
             for g in range(8):
                 line = jnp.broadcast_to(t0[an, pl.ds(g * 32 + k, 1), :], (16, WIDE))
                 line = pltpu.roll(line, 0, 1, stride=1, stride_axis=0)
-                tt[an, pl.ds(at, 16), g * WIDE : (g + 1) * WIDE] = line.astype(BF16)
+                tt[an, g // 2, pl.ds(at, 16), (g % 2) * WIDE : (g % 2 + 1) * WIDE] = line.astype(BF16)
         return carry
 
     lax.fori_loop(0, 32, spread_rows, 0)
@@ -165,31 +191,43 @@
     outer = (over == small).astype(F32).astype(BF16)
     inner = (high - ORB * over == small).astype(F32).astype(BF16)
     for an in range(4):
-        block = c_ref[an // 2, an % 2]
+        block = c_ref[an // 2][:, an % 2, :]
         left = dot_t(dot(outer, block).astype(BF16), outer)
         right = dot_t(dot(inner, block).astype(BF16), inner)
         kron[an] = (left * right).astype(BF16)
 
-    own1.wait()
-    for step in ORDER:
-        arrival(step, *leg1).wait_recv()
-
-    lower = (((lane((PAIRS, WIDE)) - 16 * (z + 7)) & 127) < 64)
-    for g in range(8):
-        near = recv1[2 * g].astype(F32)
-        far = recv1[2 * g + 1].astype(F32)
-        ga[0, :, g * WIDE : (g + 1) * WIDE] = jnp.where(lower, near, far).astype(BF16)
-        ga[1, :, g * WIDE : (g + 1) * WIDE] = jnp.where(lower, far, near).astype(BF16)
+    lower = ((lane((PAIRS, WIDE)) - 16 * (z + 7)) & 127) < 64
+    for turn in (2, 1, 3, 0):
+        part = lax.rem(z // 2 + turn, 4)
+        for i in range(4):
+            there = 4 * part + i
+
+            def wait_there():
+                pltpu.make_async_remote_copy(
+                    send1.at[there], recv1.at[there], send1_sem.at[there], recv1_sem.at[there],
+                    device_id={"mom": there}, device_id_type=MESH,
+                ).wait_recv()
+
+            if turn:
+                wait_there()
+            else:
+                pl.when(there != m)(wait_there)
+        if not turn:
+            own1.wait()
+        for g in range(2):
+            near = recv1[4 * part + 2 * g].astype(F32)
+            far = recv1[4 * part + 2 * g + 1].astype(F32)
+            ga[0, :, g * WIDE : (g + 1) * WIDE] = jnp.where(lower, near, far).astype(BF16)
+            ga[1, :, g * WIDE : (g + 1) * WIDE] = jnp.where(lower, far, near).astype(BF16)
+        for an in range(4):
+            term = dot_t(ga[nb_ref[an // 2, an % 2]], tt[an, part])
+            acc[an] = term if turn == 2 else acc[an] + term
 
     done = []
     for a in range(2):
-        total = None
-        for n in range(2):
-            an = 2 * a + n
-            conv = dot_t(ga[nb_ref[a, n]], tt[an]).astype(BF16)
-            term = dot(kron[an], conv)
-            total = term if total is None else total + term
-        done.append(total)
+        done.append(
+            dot(kron[2 * a], acc[2 * a].astype(BF16)) + dot(kron[2 * a + 1], acc[2 * a + 1].astype(BF16))
+        )
 
     place2 = lane((HALF, WIDE)) >> 4
     for g in range(4):
@@ -227,22 +265,36 @@
 
 def local(greens, phonon_kernel, coupling, neighbours, transfer_table, *, nen):
     vmem = pl.BlockSpec(memory_space=pltpu.VMEM)
+    hbm = pl.BlockSpec(memory_space=pltpu.HBM)
+    arguments = (
+        greens.transpose(0, 1, 3, 4, 2, 5).reshape(2, 2, PAIRS, 2, WIDE),
+        phonon_kernel.transpose(1, 2, 3, 0).reshape(64, 32),
+        coupling.transpose(0, 2, 1, 3),
+        neighbours,
+        transfer_table,
+    )
     out = pl.pallas_call(
         functools.partial(kernel, nen),
         out_shape=jax.ShapeDtypeStruct((2, 2, 2, PAIRS, WIDE), BF16),
-        in_specs=[vmem, vmem, vmem, pl.BlockSpec(memory_space=pltpu.SMEM), vmem],
+        in_specs=[hbm] * 5,
         out_specs=vmem,
         scratch_shapes=[
+            pltpu.VMEM((2, 2, PAIRS, 2, WIDE), BF16),
+            pltpu.VMEM((64, 32), BF16),
+            pltpu.VMEM((2, ORB, 2, ORB), BF16),
+            pltpu.SMEM((2, 2), I32),
+            pltpu.VMEM((32, 32), I32),
             pltpu.VMEM((2, 4, PAIRS, WIDE), F32),
             pltpu.VMEM((16, PAIRS, WIDE), BF16),
             pltpu.VMEM((16, PAIRS, WIDE), BF16),
             pltpu.VMEM((PAIRS, WIDE), BF16),
             pltpu.VMEM((PAIRS, WIDE), BF16),
-            pltpu.VMEM((2, PAIRS, 8 * WIDE), BF16),
-            pltpu.VMEM((4, 512, 8 * WIDE), BF16),
+            pltpu.VMEM((2, PAIRS, 2 * WIDE), BF16),
+            pltpu.VMEM((4, 4, 512, 2 * WIDE), BF16),
             pltpu.VMEM((2, 256, WIDE), BF16),
             pltpu.VMEM((4, 256, WIDE), F32),
             pltpu.VMEM((4, PAIRS, PAIRS), BF16),
+            pltpu.VMEM((4, PAIRS, 512), F32),
             pltpu.VMEM((16, HALF, WIDE), BF16),
             pltpu.VMEM((16, HALF, WIDE), BF16),
             pltpu.SemaphoreType.DMA((16,)),
@@ -251,11 +303,12 @@
             pltpu.SemaphoreType.DMA((16,)),
             pltpu.SemaphoreType.DMA((2,)),
             pltpu.SemaphoreType.DMA((2,)),
+            pltpu.SemaphoreType.DMA((5,)),
         ],
         compiler_params=pltpu.CompilerParams(
-            collective_id=0, has_side_effects=True, vmem_limit_bytes=32 * 2**20
+            collective_id=0, has_side_effects=True, vmem_limit_bytes=67_043_328
         ),
-    )(greens, phonon_kernel.reshape(32, 64), coupling, neighbours, transfer_table)
+    )(*arguments)
     return out.reshape(greens.shape)
 
 

time: 39.7 us -> 36.4 us (0.917)
  the two profiles are of different devices: /device:TPU:16 before, /device:TPU:1 now
where the time goes in v2:
time: 36.4 us; the launch traced here: 36.2 us
  Pallas kernels  34.2 us (94%)
  local copies, waits for them, and re-layouts  1.9 us (5%)
    pallas_call x1, Pallas kernels, local(): pl.pallas_call(functools.partial(kernel, nen), out_shape=jax.ShapeDtypeSt...  34.2 us
    pallas_call x1, local copies, waits for them, and re-layouts, local(): pl.pallas_call(functools.partial(kernel, nen), out_shape=jax.ShapeDtypeSt...  1.9 us

profile of v2, /device:TPU:1, one launch (start us, length us, event | category | flops | bytes accessed | tf_op | source)
XLA Modules:
  0.0 36.2 jit_solution(14929548808602496436)
XLA Ops:
  0.0 34.2 %shard_map.55 = bf16[2,2,2,144,128]{4,3,2,1,0:T(8,128)(2,1)} custom-call(bf16[2,2,144,2,128]{4,3,2,1,0:T(2,128)(2,1)} %bitcast.8, bf16[64,32]{1,0:T(8,128)(2,1)} %bitcast.9, bf16[2,12,2,12]{3,2,1,0:T(2,128)(2,1)} %bitcast.10, s32[2,2]{1,0:T(2,128)} %nb_hbm.1, s32[32,32]{1,0:T(8,128)} %t_hbm.1), custom_call_target="tpu_custom_call" | custom-call | tf_op jit(solution)/shard_map/pallas_call | solution.py:276
  34.3 1.9 %copy.7 = bf16[2,2,2,144,128]{4,2,3,1,0:T(2,128)(2,1)} copy(bf16[2,2,2,144,128]{4,3,2,1,0:T(8,128)(2,1)} %shard_map.55) | data formatting | bytes 589824 | tf_op jit(solution)/shard_map/pallas_call | solution.py:276

commit v3 on v2

v3 whole, which is shorter than its diff:
```python
import functools

import jax
import jax.numpy as jnp
from jax import lax
from jax.experimental import pallas as pl
from jax.experimental.pallas import tpu as pltpu
from jax.sharding import PartitionSpec as P

MESH = pl.DeviceIdType.MESH
F32 = jnp.float32
BF16 = jnp.bfloat16
I32 = jnp.int32

ORB = 12
PAIRS = 144
HALF = 72
WIDE = 128
LOWEST = 6
OPEN = 0
AROUND = (4, 3, 5, 2, 6, 1, 7, 0)


def order(z):
    return 4 * (z % 2) + (z // 2 + 1) % 4


def lane(shape):
    return lax.broadcasted_iota(I32, shape, len(shape) - 1)


def row(shape):
    return lax.broadcasted_iota(I32, shape, len(shape) - 2)


def pick(index, choices):
    out = choices[-1]
    for value in range(len(choices) - 2, -1, -1):
        out = jnp.where(index == value, choices[value], out)
    return out


def dot(a, b):
    return jnp.dot(a, b, preferred_element_type=F32)


def dot_t(a, b):
    return lax.dot_general(a, b, (((1,), (1,)), ((), ())), preferred_element_type=F32)


def kernel(
    nen, g_hbm, ph_hbm, c_hbm, nb_hbm, t_hbm, out_ref,
    g_ref, ph_ref, c_ref, nb_ref, t_ref,
    yt, parcel, lows, highs, ga, tt, ohs, t0, kron, acc, send2, recv2,
    home_sem, below_sem, low_sem, high_sem, pass_sem, send2_sem, recv2_sem, load_sems, open_sem,
):
    m = lax.axis_index("mom")
    q = lax.axis_index("en")
    z = m // 2
    w = order(z)
    x = m % 2
    core = q % 2
    pair = q // 2
    pairs = nen // 2
    chunk = lax.rem(2 * w + core, 8)
    holder = w // 4

    def place_of(there, pair_there, core_there):
        return {"mom": there, "en": 2 * pair_there + core_there}

    barrier = pltpu.get_barrier_semaphore()

    def greet(there, pair_there, core_there):
        pl.semaphore_signal(
            barrier, inc=1, device_id=place_of(there, pair_there, core_there), device_id_type=MESH
        )

    after = lax.rem(pair + 1, pairs)
    before = lax.rem(pair + pairs - 1, pairs)
    for step in range(1, 16):
        for c in range(2):
            greet(lax.rem(m + step, 16), pair, c)
    greet(m, pair, 1 - core)

    beside = jnp.where(core == 0, before, after)
    greet(m, beside, 1 - core)

    loads = [
        pltpu.make_async_copy(there, here, load_sems.at[i])
        for i, (there, here) in enumerate(
            [(g_hbm, g_ref), (ph_hbm, ph_ref), (c_hbm, c_ref), (nb_hbm, nb_ref), (t_hbm, t_ref)]
        )
    ]
    for load in loads:
        load.start()
    loads[0].wait()

    for c in range(4):
        both = g_ref[c % 2, lax.rem(c // 2 + x, 2)].astype(F32)
        for r in range(2):
            block = both[:, r, :]
            yt[r, c] = pltpu.roll(block, 32 * c, 1) if c else block

    place = lane((HALF, WIDE)) >> 4
    for r in range(2):
        for g in range(8):
            at = ((place + (8 - g)) & 7) >> 1
            upper = pick(at, [yt[r, c, :HALF, :] for c in range(4)])
            lower = pick(at, [yt[r, c, HALF:, :] for c in range(4)])
            parcel[r, g] = jnp.where(((place + g) & 1) == 0, upper, pltpu.roll(lower, 16, 1)).astype(BF16)

    for load in loads[1:]:
        load.wait()
    table = t_ref[...].astype(F32).astype(BF16)
    kk = row((32, WIDE))
    for v in range(2):
        for g in range(8):
            slot = lane((32, WIDE)) >> 5
            if v:
                slot = slot ^ 2
            spread = (kk == slot + 4 * g).astype(F32).astype(BF16)
            wanted = (lane((32, WIDE)) & 31).astype(F32)
            ohs[v, g * 32 : (g + 1) * 32, :] = (dot(table, spread) == wanted).astype(F32).astype(BF16)

    shifted = (lane((WIDE, WIDE)) - 16 * (chunk + 7)) & 127
    slot_match = (row((WIDE, WIDE)) >> 5) == (shifted >> 5)
    lag_at = ((lane((64, WIDE)) - 16 * (chunk + 7)) & 31)
    same = (row((32, 32)) == lane((32, 32))).astype(F32).astype(BF16)
    kernels = dot_t(same, ph_ref[...]).astype(BF16)
    for an in range(4):
        select = jnp.where(row((64, WIDE)) == 16 * an + 16 - lag_at, 1.0, 0.0)
        select = jnp.where(lag_at == 0, 0.0, jnp.where(lag_at > 16, 0.0, select)).astype(BF16)
        lags = dot(kernels, select)
        lags = jnp.concatenate([lags] * 4, axis=0)
        lags = jnp.where(slot_match, lags, 0.0).astype(BF16)
        t0[an] = dot(ohs[nb_ref[an // 2, an % 2]], lags)

    pl.semaphore_wait(barrier, 32)

    @pl.when(jnp.logical_and(core == 0, pair != 0))
    def _():
        pl.semaphore_signal(open_sem, inc=1, device_id=place_of(m, before, 1), device_id_type=MESH)

    def remote(source, target, send_sem, recv_sem, there):
        return pltpu.make_async_remote_copy(
            source, target, send_sem, recv_sem, device_id=there, device_id_type=MESH
        )

    def send_high(there, r, c):
        g = lax.rem(2 * order(there) + c, 8)
        return remote(
            parcel.at[r, g], highs.at[m], home_sem.at[r, g], high_sem.at[m], place_of(2 * there + r, pair, c)
        )

    def send_low(there, r):
        g = (2 * order(there) + 7) % 8
        return remote(
            parcel.at[r, g], lows.at[m], below_sem.at[r, g], low_sem.at[m],
            place_of(2 * there + r, after if isinstance(there, int) else pair, 0),
        )

    def first_leg(act, own):
        for turn, dz in enumerate(AROUND):
            there = lax.rem(z + dz, 8)
            holds_high = order(there) // 4 == core
            holds_low = jnp.logical_and(lax.rem(order(there) + 7, 8) // 4 == core, order(there) != 0)
            for dx in (1, 0):
                r = lax.rem(x + dx, 2)
                same = dz == 0 and dx == 0

                @pl.when(holds_high)
                def _():
                    for c in range(2):
                        if same:
                            pl.when(core != c)(lambda c=c: act(send_high(there, r, c)))
                        else:
                            act(send_high(there, r, c))

                @pl.when(jnp.logical_and(holds_low, core == 1) if same else holds_low)
                def _():
                    act(send_low(there, r))

            if turn == OPEN:

                @pl.when(jnp.logical_and(core == 1, pair != pairs - 1))
                def _():
                    if own:
                        pl.semaphore_wait(open_sem, 1)
                    for r in range(2):
                        act(send_low(LOWEST, r))

        if own:

            @pl.when(holder == core)
            def _():
                pltpu.make_async_copy(parcel.at[x, chunk], highs.at[m], high_sem.at[m]).start()

            @pl.when(jnp.logical_and(core == 0, jnp.logical_and(w > 0, w < 5)))
            def _():
                pltpu.make_async_copy(parcel.at[x, lax.rem(2 * w + 7, 8)], lows.at[m], low_sem.at[m]).start()

    first_leg(lambda copy: copy.start(), True)

    def spread_rows(k, carry):
        at = pl.multiple_of((k // 8) * 128 + lax.rem(k + chunk, 8) * 16, 16)
        for an in range(4):
            for g in range(8):
                line = jnp.broadcast_to(t0[an, pl.ds(g * 32 + k, 1), :], (16, WIDE))
                line = pltpu.roll(line, 0, 1, stride=1, stride_axis=0)
                tt[an, g // 2, pl.ds(at, 16), (g % 2) * WIDE : (g % 2 + 1) * WIDE] = line.astype(BF16)
        return carry

    lax.fori_loop(0, 32, spread_rows, 0)

    high = row((PAIRS, ORB))
    small = lane((PAIRS, ORB))
    over = jnp.zeros((PAIRS, ORB), I32)
    for i in range(1, ORB):
        over += (high >= ORB * i).astype(I32)
    outer = (over == small).astype(F32).astype(BF16)
    inner = (high - ORB * over == small).astype(F32).astype(BF16)
    for an in range(4):
        block = c_ref[an // 2][:, an % 2, :]
        left = dot_t(dot(outer, block).astype(BF16), outer)
        right = dot_t(dot(inner, block).astype(BF16), inner)
        kron[an] = (left * right).astype(BF16)

    start = jnp.logical_and(jnp.logical_and(w == 0, core == 0), pair == 0)

    def passed_on(there):
        return remote(
            highs.at[there], lows.at[there], pass_sem.at[there], low_sem.at[there], place_of(m, pair, 1)
        )

    def arrived(buffer, sem, there):
        pltpu.make_async_copy(buffer.at[there], buffer.at[there], sem.at[there]).wait()

    even = ((place + chunk) & 1) == 1
    first_half = ((lane((PAIRS, WIDE)) - 16 * (chunk + 7)) & 127) < 64

    def merged(there):
        under = jnp.where(start, 0.0, lows[there].astype(F32))
        over = highs[there].astype(F32)
        upper = jnp.where(even, under, over)
        lower = pltpu.roll(jnp.where(even, over, under), WIDE - 16, 1)
        return jnp.concatenate([upper, lower], axis=0)

    def take(part):
        for i in range(4):
            arrived(highs, high_sem, 4 * part + i)

        @pl.when(core == 0)
        def _():
            for i in range(4):
                passed_on(4 * part + i).start()

    def convolve(part, fresh):
        for i in range(4):
            pl.when(jnp.logical_not(start))(lambda i=i: arrived(lows, low_sem, 4 * part + i))
        for g in range(2):
            near = merged(4 * part + 2 * g)
            far = merged(4 * part + 2 * g + 1)
            ga[0, :, g * WIDE : (g + 1) * WIDE] = jnp.where(first_half, near, far).astype(BF16)
            ga[1, :, g * WIDE : (g + 1) * WIDE] = jnp.where(first_half, far, near).astype(BF16)
        for an in range(4):
            term = dot_t(ga[nb_ref[an // 2, an % 2]], tt[an, part])
            acc[an] = term if fresh else acc[an] + term

    parts = [lax.rem(z // 2 + turn, 4) for turn in (2, 1, 3, 0)]
    take(parts[0])
    for i in range(4):
        if i < 3:
            take(parts[i + 1])
        convolve(parts[i], i == 0)

    slot = 2 * chunk + x

    def back(there):
        return remote(
            send2.at[there], recv2.at[slot], send2_sem.at[there], recv2_sem.at[slot],
            place_of(there, pair, holder),
        )

    for g in (0, 1, 2, 3):
        done = []
        for a in range(2):
            total = None
            for an in (2 * a, 2 * a + 1):
                term = dot(kron[an], acc[an, :, g * WIDE : (g + 1) * WIDE].astype(BF16))
                total = term if total is None else total + term
            done.append(total)
        tiles = []
        for c in range(4):
            block = done[c % 2][HALF * (c // 2) : HALF * (c // 2 + 1)]
            tiles.append(pltpu.roll(block, 32 * c, 1) if c else block)
        for i in (0, 1, 2, 3):
            send2[4 * g + i] = pick(((place + 16 - chunk - 2 * i) & 7) >> 1, tiles).astype(BF16)
        for there in [4 * g + i for i in (0, 1, 2, 3)]:
            here = jnp.logical_and(m == there, holder == core)

            @pl.when(jnp.logical_not(here))
            def _():
                back(there).start()

            @pl.when(here)
            def _():
                pltpu.make_async_copy(send2.at[there], recv2.at[slot], recv2_sem.at[slot]).start()

    for there in range(16):
        arrived(recv2, recv2_sem, there)

    mine = lax.rem(m, 4)
    for r in range(2):
        blocks = [recv2[2 * b + r].astype(F32) for b in range(8)]
        halves = []
        for c in range(8):
            merged = pick((place + 16 - c - 2 * mine) & 7, blocks)
            halves.append(pltpu.roll(merged, (16 * (16 - c - 2 * mine)) & 127, 1))
        for a in range(2):
            for k in range(2):
                whole = jnp.concatenate([halves[2 * a + k], halves[4 + 2 * a + k]], axis=0)
                out_ref[k, a, r] = whole.astype(BF16)

    first_leg(lambda copy: copy.wait_send(), False)
    for there in range(16):

        @pl.when(jnp.logical_not(jnp.logical_and(m == there, holder == core)))
        def _():
            back(there).wait_send()


    @pl.when(core == 0)
    def _():
        for there in range(16):
            passed_on(there).wait_send()


def local(greens, phonon_kernel, coupling, neighbours, transfer_table, *, nen):
    vmem = pl.BlockSpec(memory_space=pltpu.VMEM)
    hbm = pl.BlockSpec(memory_space=pltpu.HBM)
    arguments = (
        greens.transpose(0, 1, 3, 4, 2, 5).reshape(2, 2, PAIRS, 2, WIDE),
        phonon_kernel.transpose(1, 2, 3, 0).reshape(64, 32),
        coupling.transpose(0, 2, 1, 3),
        neighbours,
        transfer_table,
    )
    out = pl.pallas_call(
        functools.partial(kernel, nen),
        out_shape=jax.ShapeDtypeStruct((2, 2, 2, PAIRS, WIDE), BF16),
        in_specs=[hbm] * 5,
        out_specs=vmem,
        scratch_shapes=[
            pltpu.VMEM((2, 2, PAIRS, 2, WIDE), BF16),
            pltpu.VMEM((64, 32), BF16),
            pltpu.VMEM((2, ORB, 2, ORB), BF16),
            pltpu.SMEM((2, 2), I32),
            pltpu.VMEM((32, 32), I32),
            pltpu.VMEM((2, 4, PAIRS, WIDE), F32),
            pltpu.VMEM((2, 8, HALF, WIDE), BF16),
            pltpu.VMEM((16, HALF, WIDE), BF16),
            pltpu.VMEM((16, HALF, WIDE), BF16),
            pltpu.VMEM((2, PAIRS, 2 * WIDE), BF16),
            pltpu.VMEM((4, 4, 512, 2 * WIDE), BF16),
            pltpu.VMEM((2, 256, WIDE), BF16),
            pltpu.VMEM((4, 256, WIDE), F32),
            pltpu.VMEM((4, PAIRS, PAIRS), BF16),
            pltpu.VMEM((4, PAIRS, 512), F32),
            pltpu.VMEM((16, HALF, WIDE), BF16),
            pltpu.VMEM((16, HALF, WIDE), BF16),
            pltpu.SemaphoreType.DMA((2, 8)),
            pltpu.SemaphoreType.DMA((2, 8)),
            pltpu.SemaphoreType.DMA((16,)),
            pltpu.SemaphoreType.DMA((16,)),
            pltpu.SemaphoreType.DMA((16,)),
            pltpu.SemaphoreType.DMA((16,)),
            pltpu.SemaphoreType.DMA((16,)),
            pltpu.SemaphoreType.DMA((5,)),
            pltpu.SemaphoreType.REGULAR,
        ],
        compiler_params=pltpu.CompilerParams(
            collective_id=0, has_side_effects=True, vmem_limit_bytes=32 * 2**20
        ),
    )(*(pltpu.with_memory_space_constraint(value, pltpu.HBM) for value in arguments))
    return out.reshape(greens.shape)


def solution(mesh):
    spec = P("mom", None, None, None, None, "en")
    return jax.shard_map(
        functools.partial(local, nen=mesh.shape["en"]),
        mesh=mesh,
        in_specs=(spec, P(), P(), P(), P()),
        out_specs=spec,
        check_vma=False,
    )
```

time: 36.4 us -> 33.6 us (0.923)
  Pallas kernels: 34.2 us -> 32.3 us
  local copies, waits for them, and re-layouts: 1.9 us -> 0.94 us
    pallas_call x1, Pallas kernels: 34.2 us -> 32.3 us  [local(): pl.pallas_call(functools.partial(kernel, nen), out_shape=jax.ShapeDtypeSt...]
    pallas_call x1, local copies, waits for them, and re-layouts: 1.9 us -> 0.94 us  [local(): pl.pallas_call(functools.partial(kernel, nen), out_shape=jax.ShapeDtypeSt...]
where the time goes in v3:
time: 33.6 us; the launch traced here: 33.2 us
  Pallas kernels  32.3 us (96%)
  local copies, waits for them, and re-layouts  0.94 us (3%)
    pallas_call x1, Pallas kernels, local(): pl.pallas_call(functools.partial(kernel, nen), out_shape=jax.ShapeDtypeSt...  32.3 us
    pallas_call x1, local copies, waits for them, and re-layouts, local(): pl.pallas_call(functools.partial(kernel, nen), out_shape=jax.ShapeDtypeSt...  0.94 us

profile of v3, /device:TPU:1, one launch (start us, length us, event | category | flops | bytes accessed | tf_op | source)
XLA Modules:
  0.0 33.2 jit_solution(18422494238665619781)
XLA Ops:
  0.0 32.3 %shard_map.55 = bf16[2,2,2,144,128]{4,3,2,1,0:T(8,128)(2,1)S(1)} custom-call(bf16[2,2,144,2,128]{4,3,2,1,0:T(2,128)(2,1)} %bitcast.8, bf16[64,32]{1,0:T(8,128)(2,1)} %bitcast.9, bf16[2,12,2,12]{3,2,1,0:T(2,128)(2,1)} %bitcast.10, s32[2,2]{1,0:T(2,128)} %nb_hbm.1, s32[32,32]{1,0:T(8,128)} %t_hbm.1), custom_call_target="tpu_custom_call" | custom-call | tf_op jit(solution)/shard_map/pallas_call | solution.py:348
  32.3 0.9 %copy.7 = bf16[2,2,2,144,128]{4,2,3,1,0:T(2,128)(2,1)} copy(bf16[2,2,2,144,128]{4,3,2,1,0:T(8,128)(2,1)S(1)} %shard_map.55) | data formatting | bytes 589824 | tf_op jit(solution)/shard_map/pallas_call | solution.py:348

commit v4 on v3

--- a/solution.py
+++ b/solution.py
@@ -17,7 +17,7 @@
 HALF = 72
 WIDE = 128
 LOWEST = 6
-OPEN = 0
+OPEN = 1
 AROUND = (4, 3, 5, 2, 6, 1, 7, 0)
 
 
@@ -77,13 +77,21 @@
 
     after = lax.rem(pair + 1, pairs)
     before = lax.rem(pair + pairs - 1, pairs)
-    for step in range(1, 16):
-        for c in range(2):
-            greet(lax.rem(m + step, 16), pair, c)
+    for dz in AROUND[:-1]:
+        for dx in range(2):
+            for c in range(2):
+                greet(lax.rem(z + dz, 8) * 2 + lax.rem(x + dx, 2), pair, c)
+    for c in range(2):
+        greet(2 * z + 1 - x, pair, c)
     greet(m, pair, 1 - core)
 
     beside = jnp.where(core == 0, before, after)
-    greet(m, beside, 1 - core)
+    linked = jnp.where(core == 0, pair != 0, pair != pairs - 1)
+
+    @pl.when(linked)
+    def _():
+        greet(m, beside, 1 - core)
+
 
     loads = [
         pltpu.make_async_copy(there, here, load_sems.at[i])
@@ -135,7 +143,8 @@
         lags = jnp.where(slot_match, lags, 0.0).astype(BF16)
         t0[an] = dot(ohs[nb_ref[an // 2, an % 2]], lags)
 
-    pl.semaphore_wait(barrier, 32)
+    pl.semaphore_wait(barrier, 31 + linked.astype(I32))
+
 
     @pl.when(jnp.logical_and(core == 0, pair != 0))
     def _():
@@ -267,10 +276,21 @@
             acc[an] = term if fresh else acc[an] + term
 
     parts = [lax.rem(z // 2 + turn, 4) for turn in (2, 1, 3, 0)]
+    lagging = jnp.logical_and(w == 0, core == 0)
     take(parts[0])
+
+    @pl.when(lagging)
+    def _():
+        for i in range(1, 4):
+            take(parts[i])
+
     for i in range(4):
         if i < 3:
-            take(parts[i + 1])
+
+            @pl.when(jnp.logical_not(lagging))
+            def _():
+                take(parts[i + 1])
+
         convolve(parts[i], i == 0)
 
     slot = 2 * chunk + x
@@ -306,11 +326,10 @@
             def _():
                 pltpu.make_async_copy(send2.at[there], recv2.at[slot], recv2_sem.at[slot]).start()
 
-    for there in range(16):
-        arrived(recv2, recv2_sem, there)
-
     mine = lax.rem(m, 4)
     for r in range(2):
+        for b in range(8):
+            arrived(recv2, recv2_sem, 2 * b + r)
         blocks = [recv2[2 * b + r].astype(F32) for b in range(8)]
         halves = []
         for c in range(8):

time: 33.6 us -> 32.7 us (0.973)
  Pallas kernels: 32.3 us -> 31.6 us
    pallas_call x1, Pallas kernels: 32.3 us -> 31.6 us  [local(): pl.pallas_call(functools.partial(kernel, nen), out_shape=jax.ShapeDtypeSt...]
where the time goes in v4:
time: 32.7 us; the launch traced here: 32.6 us
  Pallas kernels  31.6 us (97%)
  local copies, waits for them, and re-layouts  0.94 us (3%)
    pallas_call x1, Pallas kernels, local(): pl.pallas_call(functools.partial(kernel, nen), out_shape=jax.ShapeDtypeSt...  31.6 us
    pallas_call x1, local copies, waits for them, and re-layouts, local(): pl.pallas_call(functools.partial(kernel, nen), out_shape=jax.ShapeDtypeSt...  0.94 us

profile of v4, /device:TPU:1, one launch (start us, length us, event | category | flops | bytes accessed | tf_op | source)
XLA Modules:
  0.0 32.6 jit_solution(1565197694554895104)
XLA Ops:
  0.0 31.6 %shard_map.55 = bf16[2,2,2,144,128]{4,3,2,1,0:T(8,128)(2,1)S(1)} custom-call(bf16[2,2,144,2,128]{4,3,2,1,0:T(2,128)(2,1)} %bitcast.8, bf16[64,32]{1,0:T(8,128)(2,1)} %bitcast.9, bf16[2,12,2,12]{3,2,1,0:T(2,128)(2,1)} %bitcast.10, s32[2,2]{1,0:T(2,128)} %nb_hbm.1, s32[32,32]{1,0:T(8,128)} %t_hbm.1), custom_call_target="tpu_custom_call" | custom-call | tf_op jit(solution)/shard_map/pallas_call | solution.py:367
  31.6 0.9 %copy.7 = bf16[2,2,2,144,128]{4,2,3,1,0:T(2,128)(2,1)} copy(bf16[2,2,2,144,128]{4,3,2,1,0:T(8,128)(2,1)S(1)} %shard_map.55) | data formatting | bytes 589824 | tf_op jit(solution)/shard_map/pallas_call | solution.py:367

commit v5 on v4

--- a/solution.py
+++ b/solution.py
@@ -326,6 +326,12 @@
             def _():
                 pltpu.make_async_copy(send2.at[there], recv2.at[slot], recv2_sem.at[slot]).start()
 
+    first_leg(lambda copy: copy.wait_send(), False)
+    @pl.when(core == 0)
+    def _():
+        for there in range(16):
+            passed_on(there).wait_send()
+
     mine = lax.rem(m, 4)
     for r in range(2):
         for b in range(8):
@@ -340,18 +346,11 @@
                 whole = jnp.concatenate([halves[2 * a + k], halves[4 + 2 * a + k]], axis=0)
                 out_ref[k, a, r] = whole.astype(BF16)
 
-    first_leg(lambda copy: copy.wait_send(), False)
     for there in range(16):
 
         @pl.when(jnp.logical_not(jnp.logical_and(m == there, holder == core)))
         def _():
             back(there).wait_send()
-
-
-    @pl.when(core == 0)
-    def _():
-        for there in range(16):
-            passed_on(there).wait_send()
 
 
 def local(greens, phonon_kernel, coupling, neighbours, transfer_table, *, nen):

time: 32.7 us -> 32.7 us (level)
  no operation moved by 1% of the time
where the time goes in v5:
time: 32.7 us; the launch traced here: 32.6 us
  Pallas kernels  31.7 us (97%)
  local copies, waits for them, and re-layouts  0.94 us (3%)
    pallas_call x1, Pallas kernels, local(): pl.pallas_call(functools.partial(kernel, nen), out_shape=jax.ShapeDtypeSt...  31.7 us
    pallas_call x1, local copies, waits for them, and re-layouts, local(): pl.pallas_call(functools.partial(kernel, nen), out_shape=jax.ShapeDtypeSt...  0.94 us

profile of v5, /device:TPU:1, one launch (start us, length us, event | category | flops | bytes accessed | tf_op | source)
XLA Modules:
  0.0 32.6 jit_solution(14284047924393421544)
XLA Ops:
  0.0 31.7 %shard_map.55 = bf16[2,2,2,144,128]{4,3,2,1,0:T(8,128)(2,1)S(1)} custom-call(bf16[2,2,144,2,128]{4,3,2,1,0:T(2,128)(2,1)} %bitcast.8, bf16[64,32]{1,0:T(8,128)(2,1)} %bitcast.9, bf16[2,12,2,12]{3,2,1,0:T(2,128)(2,1)} %bitcast.10, s32[2,2]{1,0:T(2,128)} %nb_hbm.1, s32[32,32]{1,0:T(8,128)} %t_hbm.1), custom_call_target="tpu_custom_call" | custom-call | tf_op jit(solution)/shard_map/pallas_call | solution.py:366
  31.7 0.9 %copy.7 = bf16[2,2,2,144,128]{4,2,3,1,0:T(2,128)(2,1)} copy(bf16[2,2,2,144,128]{4,3,2,1,0:T(8,128)(2,1)S(1)} %shard_map.55) | data formatting | bytes 589824 | tf_op jit(solution)/shard_map/pallas_call | solution.py:366

commit v6 on v5

--- a/solution.py
+++ b/solution.py
@@ -275,7 +275,7 @@
             term = dot_t(ga[nb_ref[an // 2, an % 2]], tt[an, part])
             acc[an] = term if fresh else acc[an] + term
 
-    parts = [lax.rem(z // 2 + turn, 4) for turn in (2, 1, 3, 0)]
+    parts = [lax.rem(z // 2 + turn, 4) for turn in (0, 2, 3, 1)]
     lagging = jnp.logical_and(w == 0, core == 0)
     take(parts[0])
 

time: 32.7 us -> 32.4 us (level)
  Pallas kernels: 31.7 us -> 31.1 us
    pallas_call x1, Pallas kernels: 31.7 us -> 31.1 us  [local(): pl.pallas_call(functools.partial(kernel, nen), out_shape=jax.ShapeDtypeSt...]
where the time goes in v6:
time: 32.4 us; the launch traced here: 32.1 us
  Pallas kernels  31.1 us (96%)
  local copies, waits for them, and re-layouts  0.94 us (3%)
    pallas_call x1, Pallas kernels, local(): pl.pallas_call(functools.partial(kernel, nen), out_shape=jax.ShapeDtypeSt...  31.1 us
    pallas_call x1, local copies, waits for them, and re-layouts, local(): pl.pallas_call(functools.partial(kernel, nen), out_shape=jax.ShapeDtypeSt...  0.94 us

profile of v6, /device:TPU:1, one launch (start us, length us, event | category | flops | bytes accessed | tf_op | source)
XLA Modules:
  0.0 32.1 jit_solution(355159609007342589)
XLA Ops:
  0.0 31.1 %shard_map.55 = bf16[2,2,2,144,128]{4,3,2,1,0:T(8,128)(2,1)S(1)} custom-call(bf16[2,2,144,2,128]{4,3,2,1,0:T(2,128)(2,1)} %bitcast.8, bf16[64,32]{1,0:T(8,128)(2,1)} %bitcast.9, bf16[2,12,2,12]{3,2,1,0:T(2,128)(2,1)} %bitcast.10, s32[2,2]{1,0:T(2,128)} %nb_hbm.1, s32[32,32]{1,0:T(8,128)} %t_hbm.1), custom_call_target="tpu_custom_call" | custom-call | tf_op jit(solution)/shard_map/pallas_call | solution.py:366
  31.2 0.9 %copy.7 = bf16[2,2,2,144,128]{4,2,3,1,0:T(2,128)(2,1)} copy(bf16[2,2,2,144,128]{4,3,2,1,0:T(8,128)(2,1)S(1)} %shard_map.55) | data formatting | bytes 589824 | tf_op jit(solution)/shard_map/pallas_call | solution.py:366
